TPU v7x, 32 devices: a whole 2x2x4 slice. The times are simulated.
32 devices in a mesh: gx: 2 (over y), gy: 4 (over x, core), col: 4 (over z).
Axes of the slice: x: 2, y: 2, z: 4, core: 2. Of those that a mesh axis runs over, the one named last changes fastest.
Arguments:
- vol_pts: float32 [3, 65536], P(None, ('gx', 'gy')), may hold values from 0 to 1
- surf_pts: float32 [3, 65536], P(None, 'col'), may hold values from 0 to 1
- surf_coef: float32 [3, 65536], P(None, 'col'), may hold values from -4 to 4
- vol_tile: int32 [32, 1024], P(('gx', 'gy', 'col')), may hold values from 0 to 63, as said below
- slot: int32 [32, 1024], P(('gx', 'gy', 'col')), may hold values from 0 to 127
- wanted: int32 [32, 4, 32], P(('gx', 'gy', 'col')), may hold values from 0 to 127, as said below
- live: int32 [32], P(('gx', 'gy', 'col')), may hold values from 256 to 1024, as said below
Outputs:
- displacement: float32 [3, 65536], P(None, ('gx', 'gy', 'col'))
Inputs may be any that keep to these rules, and one draw needn't show every extreme that they name: Within one device the pairs (vol_tile, slot) are distinct. `wanted`: the 32 tiles one device requests from one index of col are distinct. Only the first live[d] slots of device d are pairs; some device has all 1024 live.
All inputs are finite; a program needn't handle non-finite values.
Results may differ from a plain program's by a relative error of at most 0.0003.
Values sent between devices are 32-bit elements; how exact they have to be, the bound alone decides.
No kernel may reach another device: no remote copies, remote signals or barrier semaphores. Data moves between devices by JAX's collectives and lax.ppermute only.
A program may use at most 64 MiB of HBM per device.

v0:
```python
import functools

import jax
import jax.numpy as jnp
from jax import lax
from jax.experimental import pallas as pl
from jax.experimental.pallas import tpu as pltpu
from jax.sharding import PartitionSpec as P

TILE = 128
RADIUS = 1.2
FEATS = 32
UNROLLS = (64, 32)
KEPT = 128
AHEAD = 3
BEHIND = 6
F32, BF16, I32 = jnp.float32, jnp.bfloat16, jnp.int32


def dot(a, b, contract=((1,), (0,))):
    return lax.dot_general(a, b, (contract, ((), ())), preferred_element_type=F32)


def tile_bits(n_local):
    return n_local.bit_length()


def iota(shape, axis):
    return lax.broadcasted_iota(I32, shape, axis)


def start_all(sems, *pairs):
    copies = [pltpu.make_async_copy(a, b, sems.at[k]) for k, (a, b) in enumerate(pairs)]
    for c in copies:
        c.start()
    return copies


def sort_kernel(
    n_col, share, live_ref, vol_hbm, slot_hbm, wanted_hbm, *refs
):
    inputs, (msg_ref, *copies_of) = refs[:3], refs[3:7]
    vol_ref, slot_ref, wanted_ref, sems, far_sems = refs[7:]
    near = start_all(sems, (vol_hbm, vol_ref), (slot_hbm, slot_ref), (wanted_hbm, wanted_ref))
    far = start_all(far_sems, *zip(inputs, copies_of))
    for c in near:
        c.wait()
    rows = vol_ref.shape[0]
    req = wanted_ref.shape[2]
    slot = slot_ref[...]
    vol = vol_ref[...].astype(F32)
    position = iota((rows, TILE), 0) * TILE + iota((rows, TILE), 1)
    peer, place = slot // req, slot % req
    key = 2 * peer + (vol_ref[...] // share == peer).astype(I32)
    key = jnp.where(position < live_ref[0], key, 2 * n_col)
    keys = 2 * n_col + 2
    masks = [(key == k).astype(F32) for k in range(keys)]
    mask = jnp.concatenate(masks, 0).astype(BF16)
    ahead = (iota((TILE, TILE), 0) < iota((TILE, TILE), 1)).astype(F32).astype(BF16)
    within = dot(mask, ahead)
    count = dot(mask, jnp.ones((TILE, TILE), BF16)).astype(BF16)
    total = keys * rows
    above = (iota((total, total), 1) < iota((total, total), 0)).astype(F32).astype(BF16)
    start = dot(above, count)
    rank = within + start
    dest = masks[0] * rank[:rows]
    for k in range(1, keys):
        dest += masks[k] * rank[k * rows : (k + 1) * rows]
    dest = dest.astype(I32)
    dest_row, dest_lane = dest // TILE, dest % TILE
    table = wanted_ref[0].astype(F32)
    if n_col % 8:
        table = jnp.concatenate([table, jnp.zeros((8 - n_col % 8, req), F32)], 0)
    table = table.astype(BF16)
    out = jnp.zeros((2 * rows, TILE), F32)
    for r in range(rows):
        row = slice(r, r + 1)
        chosen = (iota((req, TILE), 0) == place[row]).astype(F32).astype(BF16)
        tiles = dot(table, chosen)
        tiles = jnp.where(iota(tiles.shape, 0) == peer[row], tiles, 0.0)
        tile = jnp.sum(tiles, 0, keepdims=True)
        here = (iota((rows, TILE), 0) == dest_row[row]).astype(F32)
        values = jnp.concatenate([here * vol[row], here * tile], 0).astype(BF16)
        lanes = (iota((TILE, TILE), 0) == dest_lane[row]).astype(F32).astype(BF16)
        out += dot(values, lanes, ((1,), (1,)))
    msg_ref[: 2 * rows] = out.astype(I32)
    even, odd = (
        jnp.concatenate([start[k * rows : k * rows + 1] for k in range(first, keys, 2)], 0)
        for first in (0, 1)
    )
    tail = jnp.where(iota(even.shape, 1) < TILE // 2, even, odd)
    pad = msg_ref.shape[0] - 2 * rows - keys // 2
    if pad:
        tail = jnp.concatenate([tail, jnp.zeros((pad, TILE), F32)], 0)
    msg_ref[2 * rows :] = tail.astype(I32)
    for c in far:
        c.wait()


def thirds(a):
    one = a.astype(BF16).astype(F32)
    two = (a - one).astype(BF16).astype(F32)
    return one, two, a - one - two


def point_features(points):
    a = (points - 0.5) * (1.0 / RADIUS)
    norm = a[0:1] * a[0:1] + a[1:2] * a[1:2] + a[2:3] * a[2:3]
    return thirds(a), jnp.concatenate(thirds(norm), 0)


def steps(tiles, body):
    step = min(32, tiles)

    def one(b, _):
        body(b * step, pl.ds(pl.multiple_of(b * step * TILE, step * TILE), step * TILE), step)
        return 0

    lax.fori_loop(0, tiles // step, one, 0)


def pad_rows(step):
    return jnp.ones((3, step * TILE), F32), jnp.zeros((FEATS - 24, step * TILE), F32)


def feature_kernel(pts_ref, surf):
    n_local = surf.shape[0] - 1

    def surface(tile, lanes, step):
        ones, blank = pad_rows(step)
        (one, two, three), norm = point_features(pts_ref[:, lanes])
        one, two, three = -2.0 * one, -2.0 * two, -2.0 * three
        rows = jnp.concatenate([one, two, one, three, one, two, norm, ones, blank], 0).astype(BF16)
        for t in range(step):
            surf[tile + t] = rows[:, t * TILE : (t + 1) * TILE].T

    steps(n_local, surface)
    surf[n_local] = jnp.zeros((TILE, FEATS), BF16)


def fill_volumes(vol_ref, vols):
    def volume(tile, lanes, step):
        ones, blank = pad_rows(step)
        (one, two, three), norm = point_features(vol_ref[:, lanes])
        rows = jnp.concatenate([one, one, two, one, three, two, ones, norm, blank], 0).astype(BF16)
        for t in range(step):
            vols[tile + t] = rows[:, t * TILE : (t + 1) * TILE]

    steps(vols.shape[0], volume)


def fill_coefs(coef_ref, coefs):
    n_local = coefs.shape[0] - 1

    def rows(tile, lanes, step):
        coef = coef_ref[:, lanes] * 4.0
        high = coef.astype(BF16).astype(F32)
        pair = jnp.concatenate([high, coef - high, jnp.zeros((2, step * TILE), F32)], 0)
        for t in range(step):
            one = pair[:, t * TILE : (t + 1) * TILE].astype(BF16)
            coefs[tile + t] = jnp.concatenate([one, one], 1)

    steps(n_local, rows)
    coefs[n_local] = jnp.zeros((8, 2 * TILE), BF16)


def main_kernel(n_col, n_local, rows, own, me_ref, *refs):
    msgs = refs[:n_col]
    surf, vols, coefs = refs[n_col : n_col + 3]
    outs, scratch = refs[n_col + 3 : -8], refs[-8:]
    packed, lists, past, now, acc, dist, kern, sem = scratch
    targets = [0] if own else range(n_col)
    if not own:
        vol_ref, coef_ref = vols, coefs
        *outs, vols, coefs = outs
    unroll = UNROLLS[own]
    group_tiles = vols.shape[0]
    bits = tile_bits(n_local)
    me = me_ref[0]
    for k, msg in enumerate(msgs):
        packed[k * rows : (k + 1) * rows] = (msg[:rows] << bits) | msg[rows : 2 * rows]
        at = n_col * rows + 2 * k
        packed[at : at + 2] = msg[pl.ds(2 * rows + me, 2)]
    copy = pltpu.make_async_copy(packed, lists, sem)
    copy.start()
    if not own:
        fill_volumes(vol_ref, vols)
        fill_coefs(coef_ref, coefs)
    acc[...] = jnp.zeros_like(acc)
    kern[unroll - BEHIND :] = jnp.zeros((BEHIND, 2 * TILE, TILE), BF16)
    copy.wait()
    bounds = []
    for k in range(n_col):
        at = n_col * rows + 2 * k
        bounds.append((lists[at, 0], lists[at, TILE // 2], lists[at + 1, 0]))
    ends, shifts = [], []
    total = jnp.int32(0)
    for part in range(2):
        for k in range(n_col):
            first, last = bounds[k][part], bounds[k][part + 1]
            shifts.append(k * rows * TILE + first - total)
            total = total + (last - first)
            ends.append(total)
    early = jnp.maximum(ends[n_col - 1], total - KEPT)
    whole = (early + UNROLLS[0] - 1) // UNROLLS[0]
    begin = whole * UNROLLS[0] if own else 0
    trips = jnp.maximum(total - begin + unroll - 1, 0) // unroll if own else whole

    def fetch(p):
        shift = shifts[own * n_col]
        for k in range(own * n_col + 1, 2 * n_col):
            shift = jnp.where(p >= ends[k - 1], shifts[k], shift)
        valid = p < total
        at = jnp.where(valid, p + shift, 0)
        return jnp.where(valid, lists[at >> 7, at & (TILE - 1)], n_local)

    def parts(pair):
        return pair >> bits, pair & ((1 << bits) - 1)

    def move(pair, q):
        v, s = parts(pair)
        acc[v] += dot(coefs[s], kern[q])

    def distance(pair):
        v, s = parts(pair)
        return dot(surf[s], vols[v])

    def evaluate(squared, q):
        squared = jnp.minimum(jnp.maximum(squared, 1e-12), 1.0)
        radius = squared * lax.rsqrt(squared)
        falloff = 1.0 - radius
        falloff = falloff * falloff
        value = falloff * falloff * (radius + 0.25)
        high = value.astype(BF16)
        kern[q, :TILE] = high
        kern[q, TILE:] = (value - high.astype(F32)).astype(BF16)

    for q in range(unroll):
        now[q] = fetch(jnp.int32(begin + q))
    for q in range(BEHIND):
        past[q] = n_local
    for q in range(AHEAD):
        dist[q] = distance(now[q])

    def trip(h, _):
        pairs = []
        squared = [dist[q] for q in range(AHEAD)]
        for q in range(unroll):
            pairs.append(now[q])
            now[q] = fetch(begin + (h + 1) * unroll + q)
            ahead = distance(now[(q + AHEAD) % unroll])
            if q + AHEAD < unroll:
                squared.append(ahead)
            else:
                dist[q + AHEAD - unroll] = ahead
            move(pairs[q - BEHIND] if q >= BEHIND else past[q], (q - BEHIND) % unroll)
            evaluate(squared[q], q)
        for q in range(BEHIND):
            past[q] = pairs[unroll - BEHIND + q]
        return 0

    lax.fori_loop(0, trips, trip, 0)
    for q in range(BEHIND):
        move(past[q], unroll - BEHIND + q)

    share = group_tiles // n_col
    for out, k in zip(outs, targets):
        base = lax.rem(me + k, n_col) * share
        for t in range(share):
            value = acc[base + t]
            out[:, t * TILE : (t + 1) * TILE] = value[:3] + value[3:6]


def shift_right(x, k, n):
    return lax.ppermute(x, "col", [(i, (i + k) % n) for i in range(n)])


def per_device(vol_pts, surf_pts, surf_coef, vol_tile, slot, wanted, live):
    n_col = lax.axis_size("col")
    me = lax.axis_index("col").astype(I32).reshape(1)
    n_local = surf_pts.shape[1] // TILE
    group_tiles = vol_pts.shape[1] // TILE
    share = group_tiles // n_col
    list_rows = vol_tile.shape[1] // TILE
    msg_rows = -(-(2 * list_rows + n_col + 1) // 8) * 8
    packed_rows = -(-(n_col * list_rows + 2 * n_col) // 8) * 8
    smem = pl.BlockSpec(memory_space=pltpu.SMEM)
    vmem = pl.BlockSpec(memory_space=pltpu.VMEM)
    hbm = pl.BlockSpec(memory_space=pltpu.HBM)

    def stay(x):
        return pltpu.with_memory_space_constraint(x, pltpu.HBM)

    inputs = (vol_pts, surf_pts, surf_coef)
    msg, *near = pl.pallas_call(
        functools.partial(sort_kernel, n_col, share),
        out_shape=[jax.ShapeDtypeStruct((msg_rows, TILE), I32)]
        + [jax.ShapeDtypeStruct(x.shape, x.dtype) for x in inputs],
        in_specs=[smem] + [hbm] * 6,
        out_specs=[vmem] * 4,
        scratch_shapes=[
            pltpu.VMEM((list_rows, TILE), I32),
            pltpu.VMEM((list_rows, TILE), I32),
            pltpu.VMEM(wanted.shape, I32),
            pltpu.SemaphoreType.DMA((3,)),
            pltpu.SemaphoreType.DMA((3,)),
        ],
        compiler_params=pltpu.CompilerParams(vmem_limit_bytes=8 << 20),
        name="sort_pairs",
    )(live, *map(stay, (vol_tile.reshape(-1, TILE), slot.reshape(-1, TILE), wanted, *inputs)))
    msgs = [msg] + [shift_right(msg, k, n_col) for k in range(n_col - 1, 0, -1)]
    vol_near, pts_near, coef_near = near
    surf = pl.pallas_call(
        feature_kernel,
        out_shape=jax.ShapeDtypeStruct((n_local + 1, TILE, FEATS), BF16),
        in_specs=[vmem],
        out_specs=vmem,
        compiler_params=pltpu.CompilerParams(vmem_limit_bytes=16 << 20),
        name="features",
    )(pts_near)

    def sums(own, points, coefs, out_shape):
        return pl.pallas_call(
            functools.partial(main_kernel, n_col, n_local, list_rows, own),
            out_shape=out_shape,
            in_specs=[smem] + [vmem] * (n_col + 3),
            out_specs=[vmem] * len(out_shape),
            scratch_shapes=[
                pltpu.VMEM((packed_rows, TILE), I32),
                pltpu.SMEM((packed_rows, TILE), I32),
                pltpu.SMEM((BEHIND,), I32),
                pltpu.SMEM((UNROLLS[own],), I32),
                pltpu.VMEM((group_tiles, 8, TILE), F32),
                pltpu.VMEM((AHEAD, TILE, TILE), F32),
                pltpu.VMEM((UNROLLS[own], 2 * TILE, TILE), BF16),
                pltpu.SemaphoreType.DMA,
            ],
            compiler_params=pltpu.CompilerParams(vmem_limit_bytes=16 << 20),
            name="pair_sums_own" if own else "pair_sums_sent",
        )(me, *msgs, surf, points, coefs)

    part = jax.ShapeDtypeStruct((3, share * TILE), F32)
    rows = [
        jax.ShapeDtypeStruct((group_tiles, FEATS, TILE), BF16),
        jax.ShapeDtypeStruct((n_local + 1, 8, 2 * TILE), BF16),
    ]
    out, *sent, vols, coefs = sums(0, vol_near, coef_near, [part] * n_col + rows)
    sent = [shift_right(x, k, n_col) for k, x in enumerate(sent, 1)]
    for x in (*sums(1, vols, coefs, [part]), *sent):
        out = out + x
    return out


def solution(mesh):
    return jax.shard_map(
        per_device,
        mesh=mesh,
        in_specs=(
            P(None, ("gx", "gy")),
            P(None, "col"),
            P(None, "col"),
            P(("gx", "gy", "col"), None),
            P(("gx", "gy", "col"), None),
            P(("gx", "gy", "col"), None, None),
            P(("gx", "gy", "col")),
        ),
        out_specs=P(None, ("gx", "gy", "col")),
        check_vma=False,
    )
```

profile of v0, /device:TPU:12, one launch (start us, length us, event | category | flops | bytes accessed | tf_op | source)
XLA Modules:
  0.0 45.3 jit_solution(8947123274044103264)
XLA Ops:
  0.7 1.8 %sort_pairs.1 = (s32[24,128]{1,0:T(8,128)S(1)}, f32[3,8192]{1,0:T(4,128)S(1)}, f32[3,16384]{1,0:T(4,128)S(1)}, f32[3,16384]{1,0:T(4,128)S(1)}) custom-call(s32[1]{0:T(128)S(6)} %copy.8.live_ref, s32[8,128]{1,0:T(8,128)} %bitcast.3, s32[8,128]{1,0:T(8,128)} %bitcast.4, s32[1,4,32]{2,1,0:T(4,128)} %wanted_hbm.1, f32[3,8192]{1,0:T(4,128)} %refs_0_.1, ...), custom_call_target="tpu_custom_call" | custom-call | tf_op jit(solution)/shard_map/sort_pairs/pallas_call | solution.py:295
  2.5 1.6 %collective-permute-start.2 = (s32[24,128]{1,0:T(8,128)S(1)}, s32[24,128]{1,0:T(8,128)S(1)}, u32[]{:S(2)}, u32[]{:S(2)}) collective-permute-start(s32[24,128]{1,0:T(8,128)S(1)} %get-tuple-element.15.refs_0_), channel_id=1, source_target_pairs={{0,1},{1,2},{2,3},{3,0},{4,5},{5,6},{6,7},{7,4},{8,9},{9,10},{10,1... | collective-permute-start | bytes 36872 | tf_op jit(solution)/shard_map/ppermute | solution.py:275
  4.1 1.2 %collective-permute-start.1 = (s32[24,128]{1,0:T(8,128)S(1)}, s32[24,128]{1,0:T(8,128)S(1)}, u32[]{:S(2)}, u32[]{:S(2)}) collective-permute-start(s32[24,128]{1,0:T(8,128)S(1)} %get-tuple-element.15.refs_0_), channel_id=1, source_target_pairs={{0,2},{1,3},{2,0},{3,1},{4,6},{5,7},{6,4},{7,5},{8,10},{9,11},{10,... | collective-permute-start | bytes 36872 | tf_op jit(solution)/shard_map/ppermute | solution.py:275
  5.3 1.8 %collective-permute-start = (s32[24,128]{1,0:T(8,128)S(1)}, s32[24,128]{1,0:T(8,128)S(1)}, u32[]{:S(2)}, u32[]{:S(2)}) collective-permute-start(s32[24,128]{1,0:T(8,128)S(1)} %get-tuple-element.15.refs_0_), channel_id=1, source_target_pairs={{0,3},{1,0},{2,1},{3,2},{4,7},{5,4},{6,5},{7,6},{8,11},{9,8},{10,9... | collective-permute-start | bytes 36872 | tf_op jit(solution)/shard_map/ppermute | solution.py:275
  7.1 1.5 %features.1.refs_4_ = bf16[129,128,32]{2,1,0:T(8,128)(2,1)S(1)} custom-call(f32[3,16384]{1,0:T(4,128)S(1)} %get-tuple-element.16.pts_ref), custom_call_target="tpu_custom_call" | custom-call | tf_op jit(solution)/shard_map/features/pallas_call | solution.py:313
  8.6 0.0 collective-permute-done.2.refs_3_
  8.6 0.1 collective-permute-done.1.refs_2_
  8.7 0.3 collective-permute-done.refs_1_
  9.0 25.9 %pair_sums_sent.1 = (f32[3,2048]{1,0:T(4,128)S(1)}, f32[3,2048]{1,0:T(4,128)S(1)}, f32[3,2048]{1,0:T(4,128)S(1)}, f32[3,2048]{1,0:T(4,128)S(1)}, bf16[64,32,128]...) custom-call(s32[1]{0:T(128)} %bitcast.me_ref, s32[24,128]{1,0:T(8,128)S(1)} %get-tuple-element.15.refs_0_, ...), custom_call_target="tpu_custom_call" | custom-call | tf_op jit(solution)/shard_map/pair_sums_sent/pallas_call | solution.py:323
  34.9 0.1 collective-permute-start.3
  35.0 4.2 %collective-permute-start.4 = (f32[3,2048]{1,0:T(4,128)S(1)}, f32[3,2048]{1,0:T(4,128)S(1)}, u32[]{:S(2)}, u32[]{:S(2)}) collective-permute-start(f32[3,2048]{1,0:T(4,128)S(1)} %get-tuple-element.23), channel_id=1, source_target_pairs={{0,2},{1,3},{2,0},{3,1},{4,6},{5,7},{6,4},{7,5},{8,10},{9,11},{10,... | collective-permute-start | bytes 73736 | tf_op jit(solution)/shard_map/ppermute | solution.py:275
  39.1 0.0 collective-permute-start.5
  39.1 5.4 %pair_sums_own.1 = f32[3,2048]{1,0:T(4,128)S(1)} custom-call(s32[1]{0:T(128)} %bitcast.me_ref, s32[24,128]{1,0:T(8,128)S(1)} %get-tuple-element.15.refs_0_, s32[24,128]{1,0:T(8,128)S(1)} %collective-permute-done.refs_1_, s32[24,128]{1,0:T(8,128)S(1)} %collective-permute-done.1.refs_2_, s32[24,128]{1,0:T(8,128)S(1)} %collective-permute-done.2.refs_3_, ...), custom_call_target="tpu_custom_call" | custom-call | tf_op jit(solution)/shard_map/pair_sums_own/pallas_call | solution.py:323
  44.6 0.0 collective-permute-done.3
  44.6 0.0 collective-permute-done.4
  44.6 0.0 collective-permute-done.5
  44.6 0.6 %add_add_fusion = f32[3,2048]{1,0:T(4,128)} fusion(f32[3,2048]{1,0:T(4,128)S(1)} %collective-permute-done.5, f32[3,2048]{1,0:T(4,128)S(1)} %collective-permute-done.4, f32[3,2048]{1,0:T(4,128)S(1)} %collective-permute-done.3, f32[3,2048]{1,0:T(4,128)S(1)} %get-tuple-element.19, f32[3,2048]{1,0:T(4,128)S(1)} %pair_sums_own.1), kind=kLoop, calls=%fused_computation | loop fusion | flops 24576 | bytes 147456 | tf_op jit(solution)/shard_map/add | solution.py:350
Async XLA Ops:
  2.5 6.2 %collective-permute-start.2 = (s32[24,128]{1,0:T(8,128)S(1)}, s32[24,128]{1,0:T(8,128)S(1)}, u32[]{:S(2)}, u32[]{:S(2)}) collective-permute-start(s32[24,128]{1,0:T(8,128)S(1)} %get-tuple-element.15.refs_0_), channel_id=1, source_target_pairs={{0,1},{1,2},{2,3},{3,0},{4,5},{5,6},{6,7},{7,4},{8,9},{9,10},{10,1... | collective-permute-start | bytes 36872 | tf_op jit(solution)/shard_map/ppermute | solution.py:275
  4.1 4.6 %collective-permute-start.1 = (s32[24,128]{1,0:T(8,128)S(1)}, s32[24,128]{1,0:T(8,128)S(1)}, u32[]{:S(2)}, u32[]{:S(2)}) collective-permute-start(s32[24,128]{1,0:T(8,128)S(1)} %get-tuple-element.15.refs_0_), channel_id=1, source_target_pairs={{0,2},{1,3},{2,0},{3,1},{4,6},{5,7},{6,4},{7,5},{8,10},{9,11},{10,... | collective-permute-start | bytes 36872 | tf_op jit(solution)/shard_map/ppermute | solution.py:275
  5.3 3.7 %collective-permute-start = (s32[24,128]{1,0:T(8,128)S(1)}, s32[24,128]{1,0:T(8,128)S(1)}, u32[]{:S(2)}, u32[]{:S(2)}) collective-permute-start(s32[24,128]{1,0:T(8,128)S(1)} %get-tuple-element.15.refs_0_), channel_id=1, source_target_pairs={{0,3},{1,0},{2,1},{3,2},{4,7},{5,4},{6,5},{7,6},{8,11},{9,8},{10,9... | collective-permute-start | bytes 36872 | tf_op jit(solution)/shard_map/ppermute | solution.py:275
  34.9 9.7 %collective-permute-start.3 = (f32[3,2048]{1,0:T(4,128)S(1)}, f32[3,2048]{1,0:T(4,128)S(1)}, u32[]{:S(2)}, u32[]{:S(2)}) collective-permute-start(f32[3,2048]{1,0:T(4,128)S(1)} %get-tuple-element.22), channel_id=1, source_target_pairs={{0,1},{1,2},{2,3},{3,0},{4,5},{5,6},{6,7},{7,4},{8,9},{9,10},{10,1... | collective-permute-start | bytes 73736 | tf_op jit(solution)/shard_map/ppermute | solution.py:275
  35.0 9.6 %collective-permute-start.4 = (f32[3,2048]{1,0:T(4,128)S(1)}, f32[3,2048]{1,0:T(4,128)S(1)}, u32[]{:S(2)}, u32[]{:S(2)}) collective-permute-start(f32[3,2048]{1,0:T(4,128)S(1)} %get-tuple-element.23), channel_id=1, source_target_pairs={{0,2},{1,3},{2,0},{3,1},{4,6},{5,7},{6,4},{7,5},{8,10},{9,11},{10,... | collective-permute-start | bytes 73736 | tf_op jit(solution)/shard_map/ppermute | solution.py:275
  39.1 5.5 %collective-permute-start.5 = (f32[3,2048]{1,0:T(4,128)S(1)}, f32[3,2048]{1,0:T(4,128)S(1)}, u32[]{:S(2)}, u32[]{:S(2)}) collective-permute-start(f32[3,2048]{1,0:T(4,128)S(1)} %get-tuple-element.24), channel_id=1, source_target_pairs={{0,3},{1,0},{2,1},{3,2},{4,7},{5,4},{6,5},{7,6},{8,11},{9,8},{10,9... | collective-permute-start | bytes 73736 | tf_op jit(solution)/shard_map/ppermute | solution.py:275
where the time goes:
time: 44.6 us; the launch traced here: 45.3 us
  Pallas kernels  34.6 us (78%)
  starting transfers between devices  8.88 us (20%)
  between operations  0.73 us (2%)
  other arithmetic  0.64 us (1%)
    pallas_call x2, Pallas kernels, sums(): pl.pallas_call(functools.partial(main_kernel, n_col, n_local, list_rows,...  31.3 us
    ppermute x6, starting transfers between devices, shift_right(): return lax.ppermute(x, 'col', [(i, (i + k) % n) for i in range(n)])  8.88 us
    pallas_call x1, Pallas kernels, per_device(): pl.pallas_call(functools.partial(sort_kernel, n_col, share), out_shape=[j...  1.79 us
    pallas_call x1, Pallas kernels, per_device(): pl.pallas_call(feature_kernel, out_shape=jax.ShapeDtypeStruct((n_local +...  1.47 us
  transfers between devices with their start and end apart: 6, of which 2 were waited for; matrix products, arithmetic and copies ran while one was open for 0% of the time, Pallas kernels for 15%

commit v1 on v0

--- a/solution.py
+++ b/solution.py
@@ -10,7 +10,7 @@
 TILE = 128
 RADIUS = 1.2
 FEATS = 32
-UNROLLS = (64, 32)
+UNROLLS = (64, 64)
 KEPT = 128
 AHEAD = 3
 BEHIND = 6

time: 44.6 us -> 41 us (0.919)
  the two profiles are of different devices: /device:TPU:12 before, /device:TPU:0 now
where the time goes in v1:
time: 41 us; the launch traced here: 40.3 us
  Pallas kernels  27.2 us (66%)
  starting transfers between devices  10.9 us (27%)
  waiting for transfers between devices  0.86 us (2%)
  between operations  0.73 us (2%)
  other arithmetic  0.64 us (2%)
    pallas_call x2, Pallas kernels, sums(): pl.pallas_call(functools.partial(main_kernel, n_col, n_local, list_rows,...  23.9 us
    ppermute x6, starting transfers between devices, shift_right(): return lax.ppermute(x, 'col', [(i, (i + k) % n) for i in range(n)])  10.9 us
    pallas_call x1, Pallas kernels, per_device(): pl.pallas_call(functools.partial(sort_kernel, n_col, share), out_shape=[j...  1.79 us
    pallas_call x1, Pallas kernels, per_device(): pl.pallas_call(feature_kernel, out_shape=jax.ShapeDtypeStruct((n_local +...  1.47 us
    ppermute x6, waiting for transfers between devices, shift_right(): return lax.ppermute(x, 'col', [(i, (i + k) % n) for i in range(n)])  0.86 us
  transfers between devices with their start and end apart: 6, of which 1 were waited for; matrix products, arithmetic and copies ran while one was open for 0% of the time, Pallas kernels for 17%

profile of v1, /device:TPU:0, one launch (start us, length us, event | category | flops | bytes accessed | tf_op | source)
XLA Modules:
  0.0 40.3 jit_solution(14542452436550544290)
XLA Ops:
  0.7 1.8 %sort_pairs.1 = (s32[24,128]{1,0:T(8,128)S(1)}, f32[3,8192]{1,0:T(4,128)S(1)}, f32[3,16384]{1,0:T(4,128)S(1)}, f32[3,16384]{1,0:T(4,128)S(1)}) custom-call(s32[1]{0:T(128)S(6)} %copy.8.live_ref, s32[8,128]{1,0:T(8,128)} %bitcast.3, s32[8,128]{1,0:T(8,128)} %bitcast.4, s32[1,4,32]{2,1,0:T(4,128)} %wanted_hbm.1, f32[3,8192]{1,0:T(4,128)} %refs_0_.1, ...), custom_call_target="tpu_custom_call" | custom-call | tf_op jit(solution)/shard_map/sort_pairs/pallas_call | solution.py:295
  2.4 3.1 %collective-permute-start.2 = (s32[24,128]{1,0:T(8,128)S(1)}, s32[24,128]{1,0:T(8,128)S(1)}, u32[]{:S(2)}, u32[]{:S(2)}) collective-permute-start(s32[24,128]{1,0:T(8,128)S(1)} %get-tuple-element.15.refs_0_), channel_id=1, source_target_pairs={{0,1},{1,2},{2,3},{3,0},{4,5},{5,6},{6,7},{7,4},{8,9},{9,10},{10,1... | collective-permute-start | bytes 36872 | tf_op jit(solution)/shard_map/ppermute | solution.py:275
  5.5 2.6 %collective-permute-start.1 = (s32[24,128]{1,0:T(8,128)S(1)}, s32[24,128]{1,0:T(8,128)S(1)}, u32[]{:S(2)}, u32[]{:S(2)}) collective-permute-start(s32[24,128]{1,0:T(8,128)S(1)} %get-tuple-element.15.refs_0_), channel_id=1, source_target_pairs={{0,2},{1,3},{2,0},{3,1},{4,6},{5,7},{6,4},{7,5},{8,10},{9,11},{10,... | collective-permute-start | bytes 36872 | tf_op jit(solution)/shard_map/ppermute | solution.py:275
  8.1 1.3 %collective-permute-start = (s32[24,128]{1,0:T(8,128)S(1)}, s32[24,128]{1,0:T(8,128)S(1)}, u32[]{:S(2)}, u32[]{:S(2)}) collective-permute-start(s32[24,128]{1,0:T(8,128)S(1)} %get-tuple-element.15.refs_0_), channel_id=1, source_target_pairs={{0,3},{1,0},{2,1},{3,2},{4,7},{5,4},{6,5},{7,6},{8,11},{9,8},{10,9... | collective-permute-start | bytes 36872 | tf_op jit(solution)/shard_map/ppermute | solution.py:275
  9.5 1.5 %features.1.refs_4_ = bf16[129,128,32]{2,1,0:T(8,128)(2,1)S(1)} custom-call(f32[3,16384]{1,0:T(4,128)S(1)} %get-tuple-element.16.pts_ref), custom_call_target="tpu_custom_call" | custom-call | tf_op jit(solution)/shard_map/features/pallas_call | solution.py:313
  10.9 0.0 collective-permute-done.2.refs_3_
  11.0 0.0 collective-permute-done.1.refs_2_
  11.0 0.8 %collective-permute-done.refs_1_ = s32[24,128]{1,0:T(8,128)S(1)} collective-permute-done((s32[24,128]{1,0:T(8,128)S(1)}, s32[24,128]{1,0:T(8,128)S(1)}, u32[]{:S(2)}, u32[]{:S(2)}) %collective-permute-start) | collective-permute-done | bytes 12320 | tf_op jit(solution)/shard_map/ppermute | solution.py:275
  11.8 18.5 %pair_sums_sent.1 = (f32[3,2048]{1,0:T(4,128)S(1)}, f32[3,2048]{1,0:T(4,128)S(1)}, f32[3,2048]{1,0:T(4,128)S(1)}, f32[3,2048]{1,0:T(4,128)S(1)}, bf16[64,32,128]...) custom-call(s32[1]{0:T(128)} %bitcast.me_ref, s32[24,128]{1,0:T(8,128)S(1)} %get-tuple-element.15.refs_0_, ...), custom_call_target="tpu_custom_call" | custom-call | tf_op jit(solution)/shard_map/pair_sums_sent/pallas_call | solution.py:323
  30.3 0.1 collective-permute-start.3
  30.4 3.6 %collective-permute-start.4 = (f32[3,2048]{1,0:T(4,128)S(1)}, f32[3,2048]{1,0:T(4,128)S(1)}, u32[]{:S(2)}, u32[]{:S(2)}) collective-permute-start(f32[3,2048]{1,0:T(4,128)S(1)} %get-tuple-element.23), channel_id=1, source_target_pairs={{0,2},{1,3},{2,0},{3,1},{4,6},{5,7},{6,4},{7,5},{8,10},{9,11},{10,... | collective-permute-start | bytes 73736 | tf_op jit(solution)/shard_map/ppermute | solution.py:275
  34.1 0.1 collective-permute-start.5
  34.2 5.4 %pair_sums_own.1 = f32[3,2048]{1,0:T(4,128)S(1)} custom-call(s32[1]{0:T(128)} %bitcast.me_ref, s32[24,128]{1,0:T(8,128)S(1)} %get-tuple-element.15.refs_0_, s32[24,128]{1,0:T(8,128)S(1)} %collective-permute-done.refs_1_, s32[24,128]{1,0:T(8,128)S(1)} %collective-permute-done.1.refs_2_, s32[24,128]{1,0:T(8,128)S(1)} %collective-permute-done.2.refs_3_, ...), custom_call_target="tpu_custom_call" | custom-call | tf_op jit(solution)/shard_map/pair_sums_own/pallas_call | solution.py:323
  39.6 0.0 collective-permute-done.3
  39.6 0.0 collective-permute-done.4
  39.6 0.0 collective-permute-done.5
  39.6 0.6 %add_add_fusion = f32[3,2048]{1,0:T(4,128)} fusion(f32[3,2048]{1,0:T(4,128)S(1)} %collective-permute-done.5, f32[3,2048]{1,0:T(4,128)S(1)} %collective-permute-done.4, f32[3,2048]{1,0:T(4,128)S(1)} %collective-permute-done.3, f32[3,2048]{1,0:T(4,128)S(1)} %get-tuple-element.19, f32[3,2048]{1,0:T(4,128)S(1)} %pair_sums_own.1), kind=kLoop, calls=%fused_computation | loop fusion | flops 24576 | bytes 147456 | tf_op jit(solution)/shard_map/add | solution.py:350
Async XLA Ops:
  2.4 8.5 %collective-permute-start.2 = (s32[24,128]{1,0:T(8,128)S(1)}, s32[24,128]{1,0:T(8,128)S(1)}, u32[]{:S(2)}, u32[]{:S(2)}) collective-permute-start(s32[24,128]{1,0:T(8,128)S(1)} %get-tuple-element.15.refs_0_), channel_id=1, source_target_pairs={{0,1},{1,2},{2,3},{3,0},{4,5},{5,6},{6,7},{7,4},{8,9},{9,10},{10,1... | collective-permute-start | bytes 36872 | tf_op jit(solution)/shard_map/ppermute | solution.py:275
  5.5 5.4 %collective-permute-start.1 = (s32[24,128]{1,0:T(8,128)S(1)}, s32[24,128]{1,0:T(8,128)S(1)}, u32[]{:S(2)}, u32[]{:S(2)}) collective-permute-start(s32[24,128]{1,0:T(8,128)S(1)} %get-tuple-element.15.refs_0_), channel_id=1, source_target_pairs={{0,2},{1,3},{2,0},{3,1},{4,6},{5,7},{6,4},{7,5},{8,10},{9,11},{10,... | collective-permute-start | bytes 36872 | tf_op jit(solution)/shard_map/ppermute | solution.py:275
  8.1 3.7 %collective-permute-start = (s32[24,128]{1,0:T(8,128)S(1)}, s32[24,128]{1,0:T(8,128)S(1)}, u32[]{:S(2)}, u32[]{:S(2)}) collective-permute-start(s32[24,128]{1,0:T(8,128)S(1)} %get-tuple-element.15.refs_0_), channel_id=1, source_target_pairs={{0,3},{1,0},{2,1},{3,2},{4,7},{5,4},{6,5},{7,6},{8,11},{9,8},{10,9... | collective-permute-start | bytes 36872 | tf_op jit(solution)/shard_map/ppermute | solution.py:275
  30.3 9.3 %collective-permute-start.3 = (f32[3,2048]{1,0:T(4,128)S(1)}, f32[3,2048]{1,0:T(4,128)S(1)}, u32[]{:S(2)}, u32[]{:S(2)}) collective-permute-start(f32[3,2048]{1,0:T(4,128)S(1)} %get-tuple-element.22), channel_id=1, source_target_pairs={{0,1},{1,2},{2,3},{3,0},{4,5},{5,6},{6,7},{7,4},{8,9},{9,10},{10,1... | collective-permute-start | bytes 73736 | tf_op jit(solution)/shard_map/ppermute | solution.py:275
  30.4 9.2 %collective-permute-start.4 = (f32[3,2048]{1,0:T(4,128)S(1)}, f32[3,2048]{1,0:T(4,128)S(1)}, u32[]{:S(2)}, u32[]{:S(2)}) collective-permute-start(f32[3,2048]{1,0:T(4,128)S(1)} %get-tuple-element.23), channel_id=1, source_target_pairs={{0,2},{1,3},{2,0},{3,1},{4,6},{5,7},{6,4},{7,5},{8,10},{9,11},{10,... | collective-permute-start | bytes 73736 | tf_op jit(solution)/shard_map/ppermute | solution.py:275
  34.1 5.5 %collective-permute-start.5 = (f32[3,2048]{1,0:T(4,128)S(1)}, f32[3,2048]{1,0:T(4,128)S(1)}, u32[]{:S(2)}, u32[]{:S(2)}) collective-permute-start(f32[3,2048]{1,0:T(4,128)S(1)} %get-tuple-element.24), channel_id=1, source_target_pairs={{0,3},{1,0},{2,1},{3,2},{4,7},{5,4},{6,5},{7,6},{8,11},{9,8},{10,9... | collective-permute-start | bytes 73736 | tf_op jit(solution)/shard_map/ppermute | solution.py:275
